TPU v7x, 256 devices: a whole 4x4x8 slice. The times are simulated.
256 devices in a mesh: panel: 16 (over x, y), front: 16 (over z, core).
Axes of the slice: x: 4, y: 4, z: 8, core: 2. Of those that a mesh axis runs over, the one named last changes fastest.
Arguments:
- leaf_inv: float32 [16, 16, 768, 768], P('panel', 'front'), may hold values from -0.21875 to 0.21875
- parent_inv: float32 [16, 16, 768, 768], P('panel', 'front'), may hold values from -0.21875 to 0.21875
- up_coupling: float32 [16, 16, 384, 768], P('panel', 'front'), may hold values from -0.21875 to 0.21875
- down_coupling: float32 [16, 16, 768, 384], P('panel', 'front'), may hold values from -0.3125 to 0.3125
- interface_coupling: float32 [16, 16, 768, 512], P('panel', 'front'), may hold values from -0.25 to 0.25
- leaf_sources: float32 [16, 16, 3, 768, 128], P('panel', 'front'), may hold values from -6 to 6
- parent_sources: float32 [16, 16, 3, 768, 128], P('panel', 'front'), may hold values from -6 to 6
- parent_of: int32 [16, 16], P('panel'), may hold values from 0 to 15
- update_count: int32 [16, 16], P('panel'), may hold values from 128 to 384, as said below
- update_rows: int32 [16, 16, 384], P('panel'), may hold values from 0 to 767, as said below
Outputs:
- leaf_solution: float32 [16, 16, 3, 768, 128], P('panel', 'front')
- parent_solution: float32 [16, 16, 3, 768, 128], P('panel', 'front')
Inputs may be any that keep to these rules, and one draw needn't show every extreme that they name: `update_count`: a multiple of 128; some leaf of every panel has 384. `update_rows`: the entries of one leaf are distinct; those at or past its update_count are padding.
All inputs are finite; a program needn't handle non-finite values.
Results may differ from a plain program's by a relative error of at most 0.0003.
Values sent between devices are 32-bit elements; how exact they have to be, the bound alone decides.
A program may use at most 128 MiB of HBM per device.

v0:
```python
import jax
import jax.numpy as jnp
from jax import lax
from jax.sharding import PartitionSpec as P

TICKS = 3
highest_precision = lax.Precision.HIGHEST


def passed_along(value, axis, steps):
    count = lax.axis_size(axis)
    leading, last = (max(0, -steps), min(count, count - steps))
    return lax.ppermute(value, axis, [(source, source + steps) for source in range(leading, last)])


def product(matrix, operand):
    return jnp.dot(matrix, operand, precision=highest_precision, preferred_element_type=jnp.float32)


def local(
    leaf_inv,
    parent_inv,
    up_coupling,
    down_coupling,
    interface_coupling,
    leaf_sources,
    parent_sources,
    parent_of,
    update_count,
    update_rows,
):
    inverse = leaf_inv[0, 0]
    parent_inverse = parent_inv[0, 0]
    upward = up_coupling[0, 0]
    downward = down_coupling[0, 0]
    coupling = interface_coupling[0, 0]
    leaf_order = inverse.shape[0]
    parent_order = parent_inverse.shape[0]
    iface_rows = coupling.shape[1]
    parents = parent_of[0]
    counts = update_count[0]
    row_ids = update_rows[0]
    update_cap = row_ids.shape[1]
    myself = lax.axis_index("front")
    slot_ids = jnp.arange(update_cap, dtype=jnp.int32)[None, :]
    live_slots = slot_ids < counts[:, None]
    mine = live_slots & (parents[:, None] == myself)
    targets = jnp.where(mine, row_ids, parent_order).reshape(-1)
    own_live = lax.dynamic_index_in_dim(live_slots, myself, 0, keepdims=False)
    own_rows = lax.dynamic_index_in_dim(row_ids, myself, 0, keepdims=False)
    own_parent = lax.dynamic_index_in_dim(parents, myself, 0, keepdims=False)
    leaf_list = []
    parent_list = []
    previous = None
    for tick_index in range(TICKS):
        sources = leaf_sources[0, 0, tick_index]
        interface = None
        if tick_index > 0:
            interface = passed_along(previous[leaf_order - iface_rows :], "panel", 1)
        partial_solution = product(inverse, sources)
        if interface is not None:
            partial_solution = partial_solution + product(inverse, product(coupling, interface))
        update = jnp.where(own_live[:, None], product(upward, partial_solution), 0.0)
        everyone = lax.all_gather(update, "front", axis=0, tiled=True)
        assembled = jax.ops.segment_sum(everyone, targets, num_segments=parent_order + 1)[
            :parent_order
        ]
        solved = product(parent_inverse, parent_sources[0, 0, tick_index] - assembled)
        all_parents = lax.all_gather(solved, "front", axis=0, tiled=True)
        take_index = own_parent * parent_order + own_rows
        picked = jnp.where(own_live[:, None], jnp.take(all_parents, take_index, axis=0), 0.0)
        leaf_now = partial_solution - product(downward, picked)
        leaf_list.append(leaf_now)
        parent_list.append(solved)
        previous = leaf_now
    leaf_out = jnp.stack(leaf_list, axis=0)[None, None]
    parent_out = jnp.stack(parent_list, axis=0)[None, None]
    return (leaf_out, parent_out)


def solution(mesh):
    placed = (
        P("panel", "front", None, None),
        P("panel", "front", None, None),
        P("panel", "front", None, None),
        P("panel", "front", None, None),
        P("panel", "front", None, None),
        P("panel", "front", None, None, None),
        P("panel", "front", None, None, None),
        P("panel", None),
        P("panel", None),
        P("panel", None, None),
    )
    return jax.shard_map(
        local,
        mesh=mesh,
        in_specs=placed,
        out_specs=(P("panel", "front", None, None, None), P("panel", "front", None, None, None)),
        check_vma=False,
    )
```

profile of v0, /device:TPU:1, one launch (start us, length us, event | category | flops | bytes accessed | tf_op | source)
XLA Modules:
  0.0 501.0 jit_solution(5184536901057421567)
XLA Ops:
  8.9 3.1 fusion.14
  12.7 1.8 fusion.60
  16.0 43.4 %all-gather.7.cloned.1.call-done = f32[6144,128]{1,0:T(8,128)} async-done(((f32[384,128]{1,0:T(8,128)}), f32[6144,128]{1,0:T(8,128)}) %all-gather.7.cloned.1.call-update) | async-done | bytes 3145744 | tf_op jit(solution)/shard_map/all_gather | solution.py:64
  59.4 43.9 %scatter_custom_fusion = f32[769,128]{1,0:T(8,128)} fusion(s32[6144]{0:T(1024)} %bitcast.157, f32[6144,128]{1,0:T(8,128)} %all-gather.7.cloned.1.call-done, f32[]{:T(128)} %constant.34.clone.1), kind=kCustom, calls=%fused_computation.73 | custom fusion | flops 786432 | bytes 394240 | tf_op jit(solution)/shard_map/scatter-add | solution.py:65
  103.3 4.8 fusion.4
  110.2 42.6 %all-gather.9.cloned.1.call-done = f32[12288,128]{0,1:T(8,128)} async-done(((f32[768,128]{0,1:T(8,128)}), f32[12288,128]{0,1:T(8,128)}) %all-gather.9.cloned.1.call-update) | async-done | bytes 6291472 | tf_op jit(solution)/shard_map/all_gather | solution.py:69
  152.8 6.6 %copy.12 = f32[12288,128]{1,0:T(8,128)} copy(f32[12288,128]{0,1:T(8,128)} %all-gather.9.cloned.1.call-done) | data formatting | bytes 12582912 | tf_op jit(solution)/shard_map/all_gather | solution.py:69
  159.4 4.4 gather_fusion
  163.8 2.6 fusion.29
  167.2 3.4 collective-permute-start
  170.7 3.0 fusion.12
  173.7 2.2 collective-permute-done
  177.3 2.0 fusion.33
  180.1 1.8 fusion.57
  181.9 41.1 %all-gather.11.cloned.1.call-done = f32[6144,128]{1,0:T(8,128)} async-done(((f32[384,128]{1,0:T(8,128)}), f32[6144,128]{1,0:T(8,128)}) %all-gather.11.cloned.1.call-update) | async-done | bytes 3145744 | tf_op jit(solution)/shard_map/all_gather | solution.py:64
  223.0 43.9 %scatter_custom_fusion.1 = f32[769,128]{1,0:T(8,128)} fusion(s32[6144]{0:T(1024)} %bitcast.158, f32[6144,128]{1,0:T(8,128)} %all-gather.11.cloned.1.call-done, f32[]{:T(128)} %constant.34.clone.1), kind=kCustom, calls=%fused_computation.71 | custom fusion | flops 786432 | bytes 394240 | tf_op jit(solution)/shard_map/scatter-add | solution.py:65
  267.0 4.8 fusion.2
  272.1 44.4 %all-gather.13.cloned.1.call-done = f32[12288,128]{0,1:T(8,128)} async-done(((f32[768,128]{0,1:T(8,128)}), f32[12288,128]{0,1:T(8,128)}) %all-gather.13.cloned.1.call-update) | async-done | bytes 6291472 | tf_op jit(solution)/shard_map/all_gather | solution.py:69
  316.5 6.6 %copy.15 = f32[12288,128]{1,0:T(8,128)} copy(f32[12288,128]{0,1:T(8,128)} %all-gather.13.cloned.1.call-done) | data formatting | bytes 12582912 | tf_op jit(solution)/shard_map/all_gather | solution.py:69
  323.0 4.4 gather_fusion.1
  327.4 2.7 fusion.28
  330.9 3.3 collective-permute-start.1
  334.1 3.0 fusion.8
  337.1 2.4 collective-permute-done.1
  341.0 2.0 fusion.30
  345.6 41.1 %all-gather.15.cloned.1.call-done = f32[6144,128]{1,0:T(8,128)} async-done(((f32[384,128]{1,0:T(8,128)}), f32[6144,128]{1,0:T(8,128)}) %all-gather.15.cloned.1.call-update) | async-done | bytes 3145744 | tf_op jit(solution)/shard_map/all_gather | solution.py:64
  386.7 43.5 %scatter_custom_fusion.2 = f32[769,128]{1,0:T(8,128)S(1)} fusion(s32[6144]{0:T(1024)} %bitcast.159, f32[6144,128]{1,0:T(8,128)} %all-gather.15.cloned.1.call-done, f32[]{:T(128)} %constant.34.clone.1), kind=kCustom, calls=%fused_computation.69 | custom fusion | flops 786432 | bytes 394240 | tf_op jit(solution)/shard_map/scatter-add | solution.py:65
  430.2 4.7 fusion
  437.6 42.0 %all-gather.17.cloned.1.call-done = f32[12288,128]{0,1:T(8,128)} async-done(((f32[768,128]{0,1:T(8,128)}), f32[12288,128]{0,1:T(8,128)}) %all-gather.17.cloned.1.call-update) | async-done | bytes 6291472 | tf_op jit(solution)/shard_map/all_gather | solution.py:69
  479.6 6.6 %copy.18 = f32[12288,128]{1,0:T(8,128)} copy(f32[12288,128]{0,1:T(8,128)} %all-gather.17.cloned.1.call-done) | data formatting | bytes 12582912 | tf_op jit(solution)/shard_map/all_gather | solution.py:69
  486.2 4.5 gather_fusion.2
  490.6 2.4 fusion.27
  (57 shorter events, 17.9 us)
Async XLA Ops:
  7.2 1.7 copy-start
  7.2 52.2 %all-gather.7.cloned.1.call-start = ((), (), s32[]{:S(2)}) async-start(), calls=%async_computation | async-start | bytes 3342336 | tf_op jit(solution)/shard_map/all_gather | solution.py:64
  8.9 3.8 copy-start.1
  11.9 0.7 copy-start.5
  14.5 138.3 %all-gather.9.cloned.1.call-start = ((), (), s32[]{:S(2)}) async-start(), calls=%async_computation.1 | async-start | bytes 6684672 | tf_op jit(solution)/shard_map/all_gather | solution.py:69
  103.3 4.9 copy-start.12
  108.1 114.9 %all-gather.11.cloned.1.call-start = ((), (), s32[]{:S(2)}) async-start(), calls=%async_computation.2 | async-start | bytes 3342336 | tf_op jit(solution)/shard_map/all_gather | solution.py:64
  166.4 0.8 copy-start.8
  167.2 8.6 %copy-start.3 = (f32[1,1,768,512]{3,2,1,0:T(8,128)S(1)}, f32[1,1,768,512]{3,2,1,0:T(8,128)}, u32[]{:S(2)}) copy-start(f32[1,1,768,512]{3,2,1,0:T(8,128)} %param.16) | copy-start | bytes 4718596
  167.2 8.6 %collective-permute-start = (f32[512,128]{1,0:T(8,128)S(1)}, f32[512,128]{1,0:T(8,128)S(1)}, u32[]{:S(2)}, u32[]{:S(2)}) collective-permute-start(f32[512,128]{1,0:T(8,128)S(1)} %slice.51), channel_id=1, source_target_pairs={{0,16},{16,32},{32,48},{48,64},{64,80},{80,96},{96,112},{112,128},... | collective-permute-start | bytes 786440 | tf_op jit(solution)/shard_map/ppermute | solution.py:13
  179.3 0.7 copy-start.7
  181.9 134.6 %all-gather.13.cloned.1.call-start = ((), (), s32[]{:S(2)}) async-start(), calls=%async_computation.3 | async-start | bytes 6684672 | tf_op jit(solution)/shard_map/all_gather | solution.py:69
  271.8 114.9 %all-gather.15.cloned.1.call-start = ((), (), s32[]{:S(2)}) async-start(), calls=%async_computation.4 | async-start | bytes 3342336 | tf_op jit(solution)/shard_map/all_gather | solution.py:64
  330.1 0.7 copy-start.10
  330.9 8.6 %copy-start.4 = (f32[1,1,768,512]{3,2,1,0:T(8,128)S(1)}, f32[1,1,768,512]{3,2,1,0:T(8,128)}, u32[]{:S(2)}) copy-start(f32[1,1,768,512]{3,2,1,0:T(8,128)} %param.16) | copy-start | bytes 4718596
  330.9 8.6 %collective-permute-start.1 = (f32[512,128]{1,0:T(8,128)S(1)}, f32[512,128]{1,0:T(8,128)S(1)}, u32[]{:S(2)}, u32[]{:S(2)}) collective-permute-start(f32[512,128]{1,0:T(8,128)S(1)} %slice.53), channel_id=1, source_target_pairs={{0,16},{16,32},{32,48},{48,64},{64,80},{80,96},{96,112},{112,128},... | collective-permute-start | bytes 786440 | tf_op jit(solution)/shard_map/ppermute | solution.py:13
  343.0 0.7 copy-start.6
  345.5 134.1 %all-gather.17.cloned.1.call-start = ((), (), s32[]{:S(2)}) async-start(), calls=%async_computation.5 | async-start | bytes 6684672 | tf_op jit(solution)/shard_map/all_gather | solution.py:69
  486.1 4.5 copy-start.2
  490.6 2.4 copy-start.9
  490.6 2.4 copy-start.11
Sparse Core Ops, SparseCore 0:
  14.6 44.7 all-gather.6
  108.2 44.5 all-gather.8
  182.0 40.9 all-gather.10
  271.9 44.5 all-gather.12
  345.6 41.0 all-gather.14
  435.0 44.5 all-gather.16
where the time goes:
time: 502 us; the launch traced here: 501 us
  waiting for transfers between devices  259 us (52%)
  other arithmetic  138 us (27%)
  matrix products  43.2 us (9%)
  local copies, waits for them, and re-layouts  39 us (8%)
  between operations  14.3 us (3%)
  starting transfers between devices  7.16 us (1%)
    scatter-add x3, other arithmetic, local(): jax.ops.segment_sum(everyone, targets, num_segments=parent_order + 1)  131 us
    all_gather x3, waiting for transfers between devices, local(): all_parents = lax.all_gather(solved, 'front', axis=0, tiled=True)  129 us
    all_gather x3, waiting for transfers between devices, local(): everyone = lax.all_gather(update, 'front', axis=0, tiled=True)  126 us
    dot_general x16, matrix products, product(): jnp.dot(matrix, operand, precision=highest_precision, preferred_element_t...  43.2 us
    all_gather x3, local copies, waits for them, and re-layouts, local(): all_parents = lax.all_gather(solved, 'front', axis=0, tiled=True)  19.7 us
    gather x3, local copies, waits for them, and re-layouts, local(): jnp.take(all_parents, take_index, axis=0)  13.3 us
  transfers between devices with their start and end apart: 8, of which 8 were waited for; matrix products, arithmetic and copies ran while one was open for 2% of the time, Pallas kernels for 0%

commit v1 on v0

--- a/solution.py
+++ b/solution.py
@@ -66,7 +66,9 @@
             :parent_order
         ]
         solved = product(parent_inverse, parent_sources[0, 0, tick_index] - assembled)
-        all_parents = lax.all_gather(solved, "front", axis=0, tiled=True)
+        all_parents = jnp.concatenate(
+            lax.all_to_all(jnp.stack([solved] * lax.axis_size("front")), "front", 0, 0), axis=0
+        )
         take_index = own_parent * parent_order + own_rows
         picked = jnp.where(own_live[:, None], jnp.take(all_parents, take_index, axis=0), 0.0)
         leaf_now = partial_solution - product(downward, picked)

time: 502 us -> 798 us (1.59)
  blocking collectives: 0 us -> 145 us
  waiting for transfers between devices: 259 us -> 400 us
  starting transfers between devices: 7.16 us -> 16.8 us
    all_to_all x0 -> x2, waiting for transfers between devices: none -> 271 us  [local(): lax.all_to_all(jnp.stack([solved] * lax.axis_size('front')), 'front', 0, 0)]
    all_to_all x0 -> x1, blocking collectives: none -> 145 us  [local(): lax.all_to_all(jnp.stack([solved] * lax.axis_size('front')), 'front', 0, 0)]
    all_gather x3 -> x0, waiting for transfers between devices: 129 us -> none  [local(): all_parents = lax.all_gather(solved, 'front', axis=0, tiled=True)]
    all_gather x3 -> x0, local copies, waits for them, and re-layouts: 19.7 us -> none  [local(): all_parents = lax.all_gather(solved, 'front', axis=0, tiled=True)]
    all_to_all x0 -> x2, starting transfers between devices: none -> 9.6 us  [local(): lax.all_to_all(jnp.stack([solved] * lax.axis_size('front')), 'front', 0, 0)]
    another operation x0 -> x3, local copies, waits for them, and re-layouts: none -> 9.08 us  [local(): jnp.stack([solved] * lax.axis_size('front'))]
  transfers between devices with their start and end apart: 8 -> 7, of which waited for: 8 -> 7; matrix products, arithmetic and copies ran while one was open for 2% -> 2% of each run, Pallas kernels for 0% -> 0%
where the time goes in v1:
time: 798 us; the launch traced here: 790 us
  waiting for transfers between devices  400 us (50%)
  blocking collectives  145 us (18%)
  other arithmetic  138 us (17%)
  matrix products  42.5 us (5%)
  local copies, waits for them, and re-layouts  33.7 us (4%)
  starting transfers between devices  16.8 us (2%)
  between operations  14.2 us (2%)
    all_to_all x2, waiting for transfers between devices, local(): lax.all_to_all(jnp.stack([solved] * lax.axis_size('front')), 'front', 0, 0)  271 us
    all_to_all x1, blocking collectives, local(): lax.all_to_all(jnp.stack([solved] * lax.axis_size('front')), 'front', 0, 0)  145 us
    scatter-add x3, other arithmetic, local(): jax.ops.segment_sum(everyone, targets, num_segments=parent_order + 1)  131 us
    all_gather x3, waiting for transfers between devices, local(): everyone = lax.all_gather(update, 'front', axis=0, tiled=True)  125 us
    dot_general x16, matrix products, product(): jnp.dot(matrix, operand, precision=highest_precision, preferred_element_t...  42.5 us
  transfers between devices with their start and end apart: 7, of which 7 were waited for; matrix products, arithmetic and copies ran while one was open for 2% of the time, Pallas kernels for 0%

profile of v1, /device:TPU:1, one launch (start us, length us, event | category | flops | bytes accessed | tf_op | source)
XLA Modules:
  0.0 789.9 jit_solution(2472480792735925941)
XLA Ops:
  8.9 3.1 fusion.14
  15.9 43.4 %all-gather.4.cloned.1.call-done = f32[6144,128]{1,0:T(8,128)} async-done(((f32[384,128]{1,0:T(8,128)}), f32[6144,128]{1,0:T(8,128)}) %all-gather.4.cloned.1.call-update) | async-done | bytes 3145744 | tf_op jit(solution)/shard_map/all_gather | solution.py:64
  59.4 43.9 %scatter_custom_fusion = f32[769,128]{1,0:T(8,128)} fusion(s32[6144]{0:T(1024)} %bitcast.161, f32[6144,128]{1,0:T(8,128)} %all-gather.4.cloned.1.call-done, f32[]{:T(128)} %constant.34.clone.1), kind=kCustom, calls=%fused_computation.73 | custom fusion | flops 786432 | bytes 394240 | tf_op jit(solution)/shard_map/scatter-add | solution.py:65
  103.3 4.8 fusion.4
  110.0 4.2 stack.22
  114.3 4.8 all-to-all-start
  121.1 136.5 %all-to-all-done = f32[16,768,128]{2,1,0:T(8,128)} async-done(((f32[16,768,128]{2,1,0:T(8,128)}), f32[16,768,128]{2,1,0:T(8,128)}, u32[]{:S(2)}, u32[]{:S(2)}) %all-to-all-start) | async-done | bytes 6291488 | tf_op jit(solution)/shard_map/all_to_all | solution.py:70
  257.6 4.4 gather_fusion
  262.0 2.6 fusion.29
  265.5 3.6 collective-permute-start
  269.1 3.0 fusion.12
  274.7 2.0 fusion.33
  279.3 42.3 %all-gather.6.cloned.1.call-done = f32[6144,128]{1,0:T(8,128)} async-done(((f32[384,128]{1,0:T(8,128)}), f32[6144,128]{1,0:T(8,128)}) %all-gather.6.cloned.1.call-update) | async-done | bytes 3145744 | tf_op jit(solution)/shard_map/all_gather | solution.py:64
  321.6 43.9 %scatter_custom_fusion.1 = f32[769,128]{1,0:T(8,128)} fusion(s32[6144]{0:T(1024)} %bitcast.162, f32[6144,128]{1,0:T(8,128)} %all-gather.6.cloned.1.call-done, f32[]{:T(128)} %constant.34.clone.1), kind=kCustom, calls=%fused_computation.71 | custom fusion | flops 786432 | bytes 394240 | tf_op jit(solution)/shard_map/scatter-add | solution.py:65
  365.6 4.8 fusion.2
  370.3 1.9 copy.15
  373.9 145.2 %all_to_all.15 = f32[16,768,128]{2,1,0:T(8,128)} all-to-all(f32[16,768,128]{2,1,0:T(8,128)S(1)} %stack.24), channel_id=1, replica_groups=mesh['panel'=16,'front'=16] {'front'}, dimensions={0} | all-to-all | bytes 12582912 | tf_op jit(solution)/shard_map/all_to_all | solution.py:70
  519.1 4.4 gather_fusion.1
  523.5 2.6 fusion.28
  526.9 3.5 collective-permute-start.1
  530.4 3.0 fusion.8
  533.4 2.4 collective-permute-done.1
  537.3 2.0 fusion.30
  541.8 39.2 %all-gather.8.cloned.1.call-done = f32[6144,128]{1,0:T(8,128)} async-done(((f32[384,128]{1,0:T(8,128)}), f32[6144,128]{1,0:T(8,128)}) %all-gather.8.cloned.1.call-update) | async-done | bytes 3145744 | tf_op jit(solution)/shard_map/all_gather | solution.py:64
  581.0 43.5 %scatter_custom_fusion.2 = f32[769,128]{1,0:T(8,128)S(1)} fusion(s32[6144]{0:T(1024)} %bitcast.163, f32[6144,128]{1,0:T(8,128)} %all-gather.8.cloned.1.call-done, f32[]{:T(128)} %constant.34.clone.1), kind=kCustom, calls=%fused_computation.69 | custom fusion | flops 786432 | bytes 394240 | tf_op jit(solution)/shard_map/scatter-add | solution.py:65
  624.5 3.9 fusion
  628.6 3.2 stack.26
  631.8 4.8 all-to-all-start.2
  637.8 2.7 copy.20
  640.5 134.7 %all-to-all-done.2 = f32[16,768,128]{2,1,0:T(8,128)} async-done(((f32[16,768,128]{2,1,0:T(8,128)}), f32[16,768,128]{2,1,0:T(8,128)}, u32[]{:S(2)}, u32[]{:S(2)}) %all-to-all-start.2) | async-done | bytes 6291488 | tf_op jit(solution)/shard_map/all_to_all | solution.py:70
  775.2 4.4 gather_fusion.2
  779.6 2.4 fusion.27
  (60 shorter events, 24.2 us)
Async XLA Ops:
  7.2 1.7 copy-start
  7.2 52.2 %all-gather.4.cloned.1.call-start = ((), (), s32[]{:S(2)}) async-start(), calls=%async_computation.3 | async-start | bytes 3342336 | tf_op jit(solution)/shard_map/all_gather | solution.py:64
  8.9 3.8 copy-start.1
  11.9 0.7 copy-start.7
  114.3 4.8 copy-start.14
  114.3 143.4 %all-to-all-start = ((f32[16,768,128]{2,1,0:T(8,128)}), f32[16,768,128]{2,1,0:T(8,128)}, u32[]{:S(2)}, u32[]{:S(2)}) async-start(f32[16,768,128]{2,1,0:T(8,128)} %stack.22), calls=%async_computation | async-start | bytes 12582912 | tf_op jit(solution)/shard_map/all_to_all | solution.py:70
  119.1 202.6 %all-gather.6.cloned.1.call-start = ((), (), s32[]{:S(2)}) async-start(), calls=%async_computation.4 | async-start | bytes 3342336 | tf_op jit(solution)/shard_map/all_gather | solution.py:64
  264.7 0.8 copy-start.10
  265.5 7.8 copy-start.3
  265.5 7.8 collective-permute-start
  276.7 0.7 copy-start.9
  279.3 301.8 %all-gather.8.cloned.1.call-start = ((), (), s32[]{:S(2)}) async-start(), calls=%async_computation.5 | async-start | bytes 3342336 | tf_op jit(solution)/shard_map/all_gather | solution.py:64
  526.2 0.7 copy-start.12
  526.9 8.9 %copy-start.4 = (f32[1,1,768,512]{3,2,1,0:T(8,128)S(1)}, f32[1,1,768,512]{3,2,1,0:T(8,128)}, u32[]{:S(2)}) copy-start(f32[1,1,768,512]{3,2,1,0:T(8,128)} %param.16) | copy-start | bytes 4718596
  526.9 8.9 %collective-permute-start.1 = (f32[512,128]{1,0:T(8,128)S(1)}, f32[512,128]{1,0:T(8,128)S(1)}, u32[]{:S(2)}, u32[]{:S(2)}) collective-permute-start(f32[512,128]{1,0:T(8,128)S(1)} %slice.53), channel_id=1, source_target_pairs={{0,16},{16,32},{32,48},{48,64},{64,80},{80,96},{96,112},{112,128},... | collective-permute-start | bytes 786440 | tf_op jit(solution)/shard_map/ppermute | solution.py:13
  539.3 0.7 copy-start.8
  631.8 4.8 copy-start.5
  631.8 4.8 copy-start.6
  631.8 143.3 %all-to-all-start.2 = ((f32[16,768,128]{2,1,0:T(8,128)}), f32[16,768,128]{2,1,0:T(8,128)}, u32[]{:S(2)}, u32[]{:S(2)}) async-start(f32[16,768,128]{2,1,0:T(8,128)} %stack.26), calls=%async_computation.2 | async-start | bytes 12582912 | tf_op jit(solution)/shard_map/all_to_all | solution.py:70
  637.8 141.8 %copy-start.2 = (f32[1,1,768,384]{3,2,1,0:T(8,128)S(1)}, f32[1,1,768,384]{3,2,1,0:T(8,128)}, u32[]{:S(2)}) copy-start(f32[1,1,768,384]{3,2,1,0:T(8,128)} %param.15) | copy-start | bytes 3538948
  779.6 2.4 copy-start.11
  779.6 2.4 copy-start.13
Sparse Core Ops, SparseCore 0:
  14.6 44.7 all-gather.3
  279.4 42.2 all-gather.5
  541.9 39.0 all-gather.7
